TPU v7x, 32 devices: a whole 2x2x4 slice. The times are simulated.
32 devices in a mesh: beam: 2 (over x), rng: 16 (over z, y, core).
Axes of the slice: x: 2, y: 2, z: 4, core: 2. Of those that a mesh axis runs over, the one named last changes fastest.
Arguments:
- echoes: bfloat16 [4, 1024, 8192], P('beam', 'rng'), parts along dimension 0, may hold values from -6 to 6
- phase_code: int32 [256], replicated, may hold values from -1 to 1, as said below
Outputs:
- test_ratio: float32 [2048, 8192], P('beam', 'rng'), parts along dimension 0
There are 2 independent parts, one for each index of `beam`. A program takes and returns all parts, laid end to end along the dimension named above; an argument that names none is the same for every part. Nothing has to cross between parts.
Inputs may be any that keep to these rules, and one draw needn't show every extreme that they name: `phase_code`: each entry is -1 or +1.
All inputs are finite; a program needn't handle non-finite values.
Results may differ from a plain program's by a relative error of at most 0.0039.
Values may be sent and summed in bfloat16 or wider, within the bound.
A program may use at most 128 MiB of HBM per device.

v0:
```python
import math

import jax
import jax.numpy as jnp
from jax import lax
from jax.sharding import PartitionSpec as P

WIN_R = 33
WIN_D = 9
GUARD_R = 5
GUARD_D = 3


def extended(cells, sides, width):
    for axis, dim in sides:
        count = lax.axis_size(axis)
        ends = count - 1
        head = lax.slice_in_dim(cells, 0, width, axis=dim)
        tail = lax.slice_in_dim(cells, cells.shape[dim] - width, cells.shape[dim], axis=dim)
        cells = jnp.concatenate(
            [
                lax.ppermute(tail, axis, [(i, (i + 1) % count) for i in range(ends)]),
                cells,
                lax.ppermute(head, axis, [((i + 1) % count, i) for i in range(ends)]),
            ],
            axis=dim,
        )
    return cells


def toeplitz_pair(phase_code):
    length = phase_code.shape[0]
    values = phase_code.astype(jnp.float32)
    padded_code = jnp.concatenate([values, jnp.zeros((length,), jnp.float32)])
    rotated = jnp.roll(padded_code, length - 1)
    repeated = jnp.tile(rotated, length + 1)[: length * (2 * length + 1)]
    rows_made = repeated.reshape(length, 2 * length + 1)[:, : 2 * length]
    return rows_made[::-1].T.astype(jnp.bfloat16)


def compress_rows(echo_rows, next_tail, filter_pair):
    length = filter_pair.shape[1]
    row_count = echo_rows.shape[0]
    cell_count = echo_rows.shape[1]
    blocks = cell_count // length
    upper_half = filter_pair[:length]
    lower_half = filter_pair[length:]
    block_rows = echo_rows.reshape(row_count * blocks, length)
    own_terms = jnp.dot(block_rows, upper_half, preferred_element_type=jnp.float32).reshape(
        row_count, blocks, length
    )
    next_terms = jnp.dot(block_rows, lower_half, preferred_element_type=jnp.float32).reshape(
        row_count, blocks, length
    )
    tail_terms = jnp.dot(next_tail, lower_half, preferred_element_type=jnp.float32).reshape(
        row_count, 1, length
    )
    result = own_terms + jnp.concatenate([next_terms[:, 1:], tail_terms], axis=1)
    return result.reshape(row_count, cell_count).astype(jnp.bfloat16)


def doppler_table(pulses):
    index_all = jnp.arange(pulses, dtype=jnp.int32)
    phase_angle = (index_all[:, None] * index_all[None, :] % pulses).astype(jnp.float32) * (
        2.0 * math.pi / pulses
    )
    window_taper = 0.5 - 0.5 * jnp.cos(
        (index_all.astype(jnp.float32) + 0.5) * (2.0 * math.pi / pulses)
    )
    cosine = window_taper[None, :] * jnp.cos(phase_angle)
    sine_part = window_taper[None, :] * jnp.sin(phase_angle)
    top_rows = jnp.concatenate([cosine, sine_part], axis=1)
    bottom_rows = jnp.concatenate([-sine_part, cosine], axis=1)
    return jnp.concatenate([top_rows, bottom_rows], axis=0).astype(jnp.bfloat16)


def power_of(table, compressed):
    pulses = compressed.shape[1]
    stacked = compressed.reshape(2 * pulses, compressed.shape[2])
    spectrum = jnp.dot(table, stacked, preferred_element_type=jnp.float32)
    return spectrum[:pulses] * spectrum[:pulses] + spectrum[pulses:] * spectrum[pulses:]


def range_sums(padded, half_width, margin):
    cell_count = padded.shape[-1] - 2 * margin
    running = padded[..., margin - half_width : margin - half_width + cell_count]
    for offset in range(margin - half_width + 1, margin + half_width + 1):
        running = running + padded[..., offset : offset + cell_count]
    return running


def slice_sums(wrapped, half_width, reach, pulses):
    running = wrapped[reach - half_width : reach - half_width + pulses]
    for offset in range(reach - half_width + 1, reach + half_width + 1):
        running = running + wrapped[offset : offset + pulses]
    return running


def cfar_ratio(padded, valid_mask):
    margin = WIN_R // 2
    reach = WIN_D // 2
    pulses = padded.shape[0]
    wrapped = jnp.concatenate([padded[pulses - reach :], padded, padded[:reach]], axis=0)
    wide_sums = range_sums(wrapped, WIN_R // 2, margin)
    guard_sums = range_sums(wrapped, GUARD_R // 2, margin)
    train_sums = slice_sums(wide_sums, WIN_D // 2, reach, pulses) - slice_sums(
        guard_sums, GUARD_D // 2, reach, pulses
    )
    train_count = (
        range_sums(valid_mask, WIN_R // 2, margin) * WIN_D
        - range_sums(valid_mask, GUARD_R // 2, margin) * GUARD_D
    )
    noise_level = train_sums / train_count[None, :]
    center_power = padded[:, margin : padded.shape[1] - margin]
    return center_power / noise_level


def corner_turn(signal):
    return lax.all_to_all(signal, "rng", split_axis=2, concat_axis=1, tiled=True)


def local(echoes, phase_code):
    filter_pair = toeplitz_pair(phase_code)
    length = phase_code.shape[0]
    local_pulses = echoes.shape[1]
    all_cells = echoes.shape[2]
    local_rows = echoes.reshape(2 * local_pulses, all_cells)
    zero_tail = jnp.zeros((2 * local_pulses, length), jnp.bfloat16)
    local_compressed = compress_rows(local_rows, zero_tail, filter_pair).reshape(
        2, local_pulses, all_cells
    )
    compressed = corner_turn(local_compressed)
    pulses = compressed.shape[1]
    cell_count = compressed.shape[2]
    table = doppler_table(pulses)
    margin = WIN_R // 2
    power_map = power_of(table, compressed)
    padded = extended(power_map, (("rng", 1),), margin)
    position = (
        lax.axis_index("rng") * cell_count
        + jnp.arange(cell_count + 2 * margin, dtype=jnp.int32)
        - margin
    )
    total_cells = cell_count * lax.axis_size("rng")
    valid_mask = ((position >= 0) & (position < total_cells)).astype(jnp.float32)
    return cfar_ratio(padded, valid_mask)


def solution(mesh):
    placed = (P("beam", "rng", None), P())
    return jax.shard_map(
        local, mesh=mesh, in_specs=placed, out_specs=P("beam", "rng"), check_vma=False
    )
```

profile of v0, /device:TPU:13, one launch (start us, length us, event | category | flops | bytes accessed | tf_op | source)
XLA Modules:
  0.0 180.7 jit_solution(8680494630458086528)
XLA Ops:
  0.0 0.7 convert_element_type.41
  0.7 0.1 concatenate.34
  0.8 0.2 tile.10
  1.0 0.6 reshape.33
  1.6 0.3 rev.3
  1.9 2.9 %reshape_reshape.3 = bf16[4096,256]{1,0:T(8,128)(2,1)S(1)} reshape(bf16[2,64,8192]{2,1,0:T(8,128)(2,1)} %param.2) | data formatting | bytes 4194304 | tf_op jit(solution)/shard_map/reshape;reshape | solution.py:48
  4.8 0.2 convolution_bitcast_fusion.2
  5.0 2.7 %convolution_bitcast_fusion = f32[4096,256]{0,1:T(8,128)} fusion(bf16[4096,256]{1,0:T(8,128)(2,1)S(1)} %reshape_reshape.3, bf16[512,256]{0,1:T(8,128)(2,1)S(1)} %bitcast.26), kind=kOutput, calls=%fused_computation.11 | convolution fusion | flops 536870912 | bytes 6422528 | tf_op jit(solution)/shard_map/dot_general | solution.py:52
  7.7 2.7 %convolution_bitcast_fusion.1 = f32[4096,256]{0,1:T(8,128)} fusion(bf16[4096,256]{1,0:T(8,128)(2,1)S(1)} %reshape_reshape.3, bf16[512,256]{0,1:T(8,128)(2,1)S(1)} %bitcast.27), kind=kOutput, calls=%fused_computation.12 | convolution fusion | flops 536870912 | bytes 6422528 | tf_op jit(solution)/shard_map/dot_general | solution.py:49
  10.4 5.6 %copy.16 = f32[4096,256]{1,0:T(8,128)} copy(f32[4096,256]{0,1:T(8,128)} %convolution_bitcast_fusion) | data formatting | bytes 8388608 | tf_op jit(solution)/shard_map/dot_general | solution.py:52
  16.0 2.8 %slice.379 = f32[128,31,256]{2,1,0:T(8,128)S(1)} slice(f32[128,32,256]{2,1,0:T(8,128)} %bitcast.23), slice={[0:128], [1:32], [0:256]} | slice | bytes 8126464 | tf_op jit(solution)/shard_map/slice | solution.py:58
  18.8 0.1 copy.17
  18.9 2.5 %pad_maximum_fusion = f32[128,32,256]{2,1,0:T(8,128)} fusion(f32[128,1,256]{2,1,0:T(1,128)S(1)} %copy.17, f32[128,31,256]{2,1,0:T(8,128)S(1)} %slice.379), kind=kLoop, calls=%fused_computation.16 | loop fusion | flops 1048576 | bytes 8388608 | tf_op jit(solution)/shard_map/concatenate | solution.py:58
  21.5 5.0 %concatenate.36 = f32[2,64,8192]{2,1,0:T(8,128)} reshape(f32[128,32,256]{2,1,0:T(8,128)} %pad_maximum_fusion) | data formatting | bytes 8388608 | tf_op jit(solution)/shard_map/concatenate | solution.py:58
  26.4 5.6 %copy.15 = f32[4096,256]{1,0:T(8,128)} copy(f32[4096,256]{0,1:T(8,128)} %convolution_bitcast_fusion.1) | data formatting | bytes 8388608 | tf_op jit(solution)/shard_map/dot_general | solution.py:49
  32.1 4.9 %reshape.34 = f32[2,64,8192]{2,1,0:T(8,128)} reshape(f32[4096,256]{1,0:T(8,128)} %copy.15) | data formatting | bytes 8388608 | tf_op jit(solution)/shard_map/reshape | solution.py:49
  37.0 3.9 %add_convert_fusion = bf16[2,64,8192]{2,1,0:T(8,128)(2,1)S(1)} fusion(f32[2,64,8192]{2,1,0:T(8,128)} %reshape.34, f32[2,64,8192]{2,1,0:T(8,128)} %concatenate.36), kind=kLoop, calls=%fused_computation.17 | loop fusion | flops 2097152 | bytes 10485760 | tf_op jit(solution)/shard_map/convert_element_type | solution.py:59
  40.9 6.9 %copy.18 = bf16[2,64,8192]{1,0,2:T(2,128)(2,1)} copy(bf16[2,64,8192]{2,1,0:T(8,128)(2,1)S(1)} %add_convert_fusion) | data formatting | bytes 4194304 | tf_op jit(solution)/shard_map/convert_element_type | solution.py:59
  47.8 7.5 %reshape.38 = bf16[16,2,32768]{2,1,0:T(2,128)(2,1)} reshape(bf16[8192,2,64]{2,1,0:T(2,128)(2,1)} %bitcast.21) | data formatting | bytes 4194304
  55.3 6.6 %all-to-all-start = ((bf16[16,2,32768]{2,1,0:T(2,128)(2,1)}), bf16[16,2,32768]{2,1,0:T(2,128)(2,1)S(1)}, u32[]{:S(2)}, u32[]{:S(2)}) async-start(bf16[16,2,32768]{2,1,0:T(2,128)(2,1)} %reshape.38), calls=%async_computation | async-start | bytes 4194304 | tf_op jit(solution)/shard_map/all_to_all | solution.py:119
  61.9 19.0 %fusion.14 = (bf16[1024,1024]{1,0:T(8,128)(2,1)}, bf16[1024,1024]{1,0:T(8,128)(2,1)}, bf16[1024,1024]{1,0:T(8,128)(2,1)}) fusion(f32[1024]{0:T(1024)S(1)} %multiply_subtract_fusion), kind=kLoop, calls=%fused_computation.24 | loop fusion | flops 20971520 | bytes 6295552 | tf_op jit(solution)/shard_map/convert.5
  80.9 28.3 %all-to-all-done = bf16[16,2,32768]{2,1,0:T(2,128)(2,1)S(1)} async-done(((bf16[16,2,32768]{2,1,0:T(2,128)(2,1)}), bf16[16,2,32768]{2,1,0:T(2,128)(2,1)S(1)}, u32[]{:S(2)}, u32[]{:S(2)}) %all-to-all-start) | async-done | bytes 2097184 | tf_op jit(solution)/shard_map/all_to_all | solution.py:119
  109.3 5.0 %reshape.39 = bf16[8192,2,64]{2,1,0:T(2,128)(2,1)} reshape(bf16[16,2,32768]{2,1,0:T(2,128)(2,1)S(1)} %all-to-all-done) | data formatting | bytes 4194304
  114.2 9.1 %copy.23 = bf16[2,64,16,512]{3,1,2,0:T(8,128)(2,1)S(1)} copy(bf16[2,64,16,512]{1,0,3,2:T(2,128)(2,1)} %bitcast.22) | data formatting | bytes 4194304 | tf_op jit(solution)/shard_map/all_to_all | solution.py:119
  123.3 10.6 %fusion = f32[2048,512]{0,1:T(8,128)S(1)} fusion(bf16[2048,512]{1,0:T(8,128)(2,1)S(1)} %bitcast.24, bf16[1024,1024]{1,0:T(8,128)(2,1)} %get-tuple-element.11, bf16[1024,1024]{1,0:T(8,128)(2,1)} %get-tuple-element.10, bf16[1024,1024]{1,0:T(8,128)(2,1)} %get-tuple-element.9), kind=kOutput, calls=%fused_computation | convolution fusion | flops 4328521728 | bytes 12582912 | tf_op jit(solution)/shard_map/dot_general | solution.py:80
  133.9 0.0 copy-start
  133.9 0.4 fusion.22
  134.4 1.5 copy-done
  135.8 3.6 %collective-permute-start = (f32[1024,16]{0,1:T(8,128)S(1)}, f32[1024,16]{0,1:T(8,128)S(1)}, u32[]{:S(2)}, u32[]{:S(2)}) collective-permute-start(f32[1024,16]{0,1:T(8,128)S(1)} %get-tuple-element.7), channel_id=1, source_target_pairs={{0,1},{1,2},{2,3},{3,4},{4,5},{5,6},{6,7},{7,8},{8,9},{9,10},{10,1... | collective-permute-start | bytes 196616 | tf_op jit(solution)/shard_map/ppermute | solution.py:22
  139.4 2.1 %collective-permute-start.1 = (f32[1024,16]{0,1:T(8,128)S(1)}, f32[1024,16]{0,1:T(8,128)S(1)}, u32[]{:S(2)}, u32[]{:S(2)}) collective-permute-start(f32[1024,16]{0,1:T(8,128)S(1)} %get-tuple-element.8), channel_id=1, source_target_pairs={{1,0},{2,1},{3,2},{4,3},{5,4},{6,5},{7,6},{8,7},{9,8},{10,9},{11,1... | collective-permute-start | bytes 196616 | tf_op jit(solution)/shard_map/ppermute | solution.py:24
  141.6 0.1 multiply_subtract_fusion.1
  141.7 0.0 collective-permute-done
  141.7 4.2 %collective-permute-done.1 = f32[1024,16]{0,1:T(8,128)S(1)} collective-permute-done((f32[1024,16]{0,1:T(8,128)S(1)}, f32[1024,16]{0,1:T(8,128)S(1)}, u32[]{:S(2)}, u32[]{:S(2)}) %collective-permute-start.1) | collective-permute-done | bytes 65568 | tf_op jit(solution)/shard_map/ppermute | solution.py:24
  145.9 0.3 pad_maximum_fusion.1
  146.2 0.0 copy-start.1
  146.2 0.1 fusion.33
  146.3 1.2 copy-done.1
  147.6 3.2 %concatenate.38 = f32[1032,544]{0,1:T(8,128)S(1)} concatenate(f32[4,544]{0,1:T(8,128)S(1)} %get-tuple-element.6, f32[1024,544]{0,1:T(8,128)} %copy-done.1, f32[4,544]{0,1:T(8,128)S(1)} %get-tuple-element.5), dimensions={0} | concatenate | bytes 4491264 | tf_op jit(solution)/shard_map/concatenate | solution.py:103
  150.7 2.3 %add_add_fusion = f32[1032,512]{0,1:T(8,128)} fusion(f32[1032,544]{0,1:T(8,128)S(1)} %concatenate.38), kind=kLoop, calls=%fused_computation.57 | loop fusion | flops 2113536 | bytes 12681216 | tf_op jit(solution)/shard_map/add | solution.py:88
  153.1 7.7 %slice_add_fusion = f32[1032,512]{0,1:T(8,128)} fusion(f32[1032,544]{0,1:T(8,128)S(1)} %concatenate.38), kind=kLoop, calls=%fused_computation.25 | loop fusion | flops 16908288 | bytes 71860224 | tf_op jit(solution)/shard_map/add | solution.py:88
  160.8 18.1 %fusion.21 = f32[1024,512]{0,1:T(8,128)S(1)} fusion(f32[1032,512]{0,1:T(8,128)} %add_add_fusion, f32[1032,512]{0,1:T(8,128)} %slice_add_fusion, f32[512]{0:T(512)S(1)} %multiply_subtract_fusion.1, f32[2048,512]{0,1:T(8,128)} %copy-done), kind=kLoop, calls=%fused_computation.61 | loop fusion | flops 8388608 | bytes 31459328 | tf_op jit(solution)/shard_map/div | solution.py:115
  178.8 1.8 %copy.21 = f32[1024,512]{1,0:T(8,128)} copy(f32[1024,512]{0,1:T(8,128)S(1)} %fusion.21) | data formatting | bytes 4194304 | tf_op jit(solution)/shard_map/div | solution.py:115
  (6 shorter events, 0.1 us)
Async XLA Ops:
  55.3 54.0 %all-to-all-start = ((bf16[16,2,32768]{2,1,0:T(2,128)(2,1)}), bf16[16,2,32768]{2,1,0:T(2,128)(2,1)S(1)}, u32[]{:S(2)}, u32[]{:S(2)}) async-start(bf16[16,2,32768]{2,1,0:T(2,128)(2,1)} %reshape.38), calls=%async_computation | async-start | bytes 4194304 | tf_op jit(solution)/shard_map/all_to_all | solution.py:119
  133.9 1.9 %copy-start = (f32[2048,512]{0,1:T(8,128)}, f32[2048,512]{0,1:T(8,128)S(1)}, u32[]{:S(2)}) copy-start(f32[2048,512]{0,1:T(8,128)S(1)} %fusion) | copy-start | bytes 12582916
  135.8 5.8 %collective-permute-start = (f32[1024,16]{0,1:T(8,128)S(1)}, f32[1024,16]{0,1:T(8,128)S(1)}, u32[]{:S(2)}, u32[]{:S(2)}) collective-permute-start(f32[1024,16]{0,1:T(8,128)S(1)} %get-tuple-element.7), channel_id=1, source_target_pairs={{0,1},{1,2},{2,3},{3,4},{4,5},{5,6},{6,7},{7,8},{8,9},{9,10},{10,1... | collective-permute-start | bytes 196616 | tf_op jit(solution)/shard_map/ppermute | solution.py:22
  139.4 6.5 %collective-permute-start.1 = (f32[1024,16]{0,1:T(8,128)S(1)}, f32[1024,16]{0,1:T(8,128)S(1)}, u32[]{:S(2)}, u32[]{:S(2)}) collective-permute-start(f32[1024,16]{0,1:T(8,128)S(1)} %get-tuple-element.8), channel_id=1, source_target_pairs={{1,0},{2,1},{3,2},{4,3},{5,4},{6,5},{7,6},{8,7},{9,8},{10,9},{11,1... | collective-permute-start | bytes 196616 | tf_op jit(solution)/shard_map/ppermute | solution.py:24
  146.2 1.4 copy-start.1
where the time goes:
time: 182 us; the launch traced here: 181 us
  local copies, waits for them, and re-layouts  64.4 us (35%)
  other arithmetic  55.1 us (30%)
  waiting for transfers between devices  32.5 us (18%)
  matrix products  16.1 us (9%)
  starting transfers between devices  12.3 us (7%)
    all_to_all x1, waiting for transfers between devices, corner_turn(): lax.all_to_all(signal, 'rng', split_axis=2, concat_axis=1, tiled=True)  28.3 us
    another operation x1, other arithmetic  19 us
    div x1, other arithmetic, cfar_ratio(): return center_power / noise_level  18.1 us
    unnamed x6, local copies, waits for them, and re-layouts  15.2 us
    dot_general x1, matrix products, power_of(): spectrum = jnp.dot(table, stacked, preferred_element_type=jnp.float32)  10.6 us
    add x2, other arithmetic, range_sums(): running = running + padded[..., offset:offset + cell_count]  10 us
    all_to_all x1, local copies, waits for them, and re-layouts, corner_turn(): lax.all_to_all(signal, 'rng', split_axis=2, concat_axis=1, tiled=True)  9.07 us
    convert_element_type x1, local copies, waits for them, and re-layouts, compress_rows(): return result.reshape(row_count, cell_count).astype(jnp.bfloat16)  6.89 us
  transfers between devices with their start and end apart: 3, of which 2 were waited for; matrix products, arithmetic and copies ran while one was open for 11% of the time, Pallas kernels for 0%

commit v1 on v0

v1 whole, which is shorter than its diff:
```python
import functools
import math

import jax
import jax.numpy as jnp
import numpy as np
from jax import lax
from jax.experimental import pallas as pl
from jax.experimental.pallas import tpu as pltpu
from jax.sharding import PartitionSpec as P

WIN_R = 33
WIN_D = 9
GUARD_R = 5
GUARD_D = 3
LANES = 128
HALO = WIN_R // 2
PACK = LANES // HALO
ROW_PAD = 8
DOPPLER_TILE = 256
CFAR_ROWS = 32
MESH = pl.DeviceIdType.MESH


def doppler_table(pulses, local_pulses):
    index_all = np.arange(pulses, dtype=np.int64)
    step = np.float32(2.0 * math.pi / pulses)
    angle = (index_all[:, None] * index_all[None, :] % pulses).astype(np.float32) * step
    taper = np.float32(0.5) - np.float32(0.5) * np.cos((index_all.astype(np.float32) + np.float32(0.5)) * step)
    cosine = taper[None, :] * np.cos(angle)
    sine = taper[None, :] * np.sin(angle)
    table = np.block([[cosine, sine], [-sine, cosine]]).astype(jnp.bfloat16)
    table = table.reshape(2 * pulses, 2, pulses // local_pulses, local_pulses)
    table = table.transpose(0, 2, 1, 3).reshape(2, pulses // DOPPLER_TILE, DOPPLER_TILE, 2 * pulses)
    return table.transpose(1, 0, 2, 3).reshape(2 * pulses, 2 * pulses)


def shifted(x, count, axis):
    size = x.shape[axis]
    return pltpu.roll(x, (-count) % size, axis)


def body(
    n, echoes_hbm, code_ref, table_hbm, out_ref,
    echoes, table, filters, sending, held, power, edge_out, edge_in,
    echo_sem, table_sem, send_sem, recv_sem, edge_send_sem, edge_recv_sem,
):
    me = lax.axis_index("rng")
    taps = code_ref.shape[1]
    rows, all_cells = echoes_hbm.shape
    cells = all_cells // n
    blocks = cells // taps
    bins = table.shape[0] // 2

    echo_copy = pltpu.make_async_copy(echoes_hbm, echoes.at[:, pl.ds(0, all_cells)], echo_sem)
    echo_copy.start()
    table_copy = pltpu.make_async_copy(table_hbm, table, table_sem)
    table_copy.start()

    barrier = pltpu.get_barrier_semaphore()

    @pl.loop(1, n)
    def _(k):
        pl.semaphore_signal(barrier, inc=1, device_id={"rng": lax.rem(me + k, n)}, device_id_type=MESH)

    row = lax.broadcasted_iota(jnp.int32, (taps, taps), 0)
    col = lax.broadcasted_iota(jnp.int32, (taps, taps), 1)
    rolled = jnp.broadcast_to(code_ref[...].astype(jnp.float32), (taps, taps))
    for bit in range((taps - 1).bit_length()):
        rolled = jnp.where((row & (1 << bit)) != 0, pltpu.roll(rolled, 1 << bit, 1), rolled)
    circulant = rolled.T
    filters[pl.ds(0, taps), :] = jnp.where(row >= col, circulant, 0.0).astype(jnp.bfloat16)
    filters[pl.ds(taps, taps), :] = jnp.where(row < col, circulant, 0.0).astype(jnp.bfloat16)
    echoes[:, pl.ds(all_cells, taps)] = jnp.zeros((rows, taps), jnp.bfloat16)

    echo_copy.wait()
    pl.semaphore_wait(barrier, n - 1)

    def compressed(owner):
        parts = [
            echoes[:, pl.ds(pl.multiple_of(owner * cells + b * taps, taps), taps)] for b in range(blocks + 1)
        ]
        pairs = jnp.concatenate(
            [jnp.concatenate(parts[:-1], axis=0), jnp.concatenate(parts[1:], axis=0)], axis=1
        )
        made = jnp.dot(pairs, filters[...], preferred_element_type=jnp.float32).astype(jnp.bfloat16)
        return [made[b * rows : (b + 1) * rows] for b in range(blocks)]

    def block_copy(slot, owner):
        return pltpu.make_async_remote_copy(
            src_ref=sending.at[owner],
            dst_ref=held.at[slot],
            send_sem=send_sem.at[owner],
            recv_sem=recv_sem.at[slot],
            device_id={"rng": owner},
            device_id_type=MESH,
        )

    @pl.loop(1, n)
    def _(k):
        owner = lax.rem(me + k, n)
        for b, part in enumerate(compressed(owner)):
            sending[owner, :, b * taps : (b + 1) * taps] = part
        block_copy(me, owner).start()

    for b, part in enumerate(compressed(me)):
        held[me, :, b * taps : (b + 1) * taps] = part

    table_copy.wait()

    @pl.loop(1, n)
    def _(k):
        block_copy(lax.rem(me + n - k, n), lax.rem(me + k, n)).wait()

    signal = held[...].reshape(n * rows, cells)

    @pl.loop(0, bins // DOPPLER_TILE)
    def _(i):
        made = jnp.dot(
            table[pl.ds(pl.multiple_of(i * 2 * DOPPLER_TILE, 2 * DOPPLER_TILE), 2 * DOPPLER_TILE), :],
            signal,
            preferred_element_type=jnp.float32,
        )
        real, imag = made[:DOPPLER_TILE], made[DOPPLER_TILE:]
        start = pl.multiple_of(i * DOPPLER_TILE + ROW_PAD, ROW_PAD)
        power[pl.ds(start, DOPPLER_TILE), pl.ds(0, cells)] = real * real + imag * imag

    group = bins // PACK
    lane = lax.broadcasted_iota(jnp.int32, (group, LANES), 1)

    def packed(first, turn):
        total = jnp.zeros((group, LANES), jnp.float32)
        for g in range(PACK):
            tile = power[pl.ds(ROW_PAD + g * group, group), pl.ds(first, LANES)]
            total = jnp.where(lane // HALO == g, pltpu.roll(tile, (g * HALO + turn) % LANES, 1), total)
        return total

    edge_out[0] = packed(0, 0)
    edge_out[1] = packed(cells - LANES, HALO)

    def edge_copy(side):
        return pltpu.make_async_remote_copy(
            src_ref=edge_out.at[side],
            dst_ref=edge_in.at[side],
            send_sem=edge_send_sem.at[side],
            recv_sem=edge_recv_sem.at[side],
            device_id={"rng": lax.rem(me + (n - 1 if side == 0 else 1), n)},
            device_id_type=MESH,
        )

    has_left, has_right = me > 0, me < n - 1

    @pl.when(has_left)
    def _():
        edge_copy(0).start()

    @pl.when(has_right)
    def _():
        edge_copy(1).start()

    @pl.when(has_right)
    def _():
        edge_copy(0).wait_recv()

    @pl.when(jnp.logical_not(has_right))
    def _():
        edge_in[0] = jnp.zeros((group, LANES), jnp.float32)

    @pl.when(has_left)
    def _():
        edge_copy(1).wait_recv()

    @pl.when(jnp.logical_not(has_left))
    def _():
        edge_in[1] = jnp.zeros((group, LANES), jnp.float32)

    after, before = edge_in[0], edge_in[1]
    for g in range(PACK):
        tile = jnp.where(
            lane < HALO,
            pltpu.roll(after, (-g * HALO) % LANES, 1),
            jnp.where(lane >= LANES - HALO, pltpu.roll(before, (-g * HALO - HALO) % LANES, 1), 0.0),
        )
        power[pl.ds(ROW_PAD + g * group, group), pl.ds(cells, LANES)] = tile
    power[pl.ds(0, ROW_PAD), :] = power[pl.ds(bins, ROW_PAD), :]
    power[pl.ds(bins + ROW_PAD, ROW_PAD), :] = power[pl.ds(ROW_PAD, ROW_PAD), :]

    position = me * cells + lax.broadcasted_iota(jnp.int32, (1, cells), 1)

    def inside(half):
        return jnp.minimum(position + half, all_cells - 1) - jnp.maximum(position - half, 0) + 1

    count = inside(WIN_R // 2) * WIN_D - inside(GUARD_R // 2) * GUARD_D
    inverse_count = 1.0 / count.astype(jnp.float32)

    @pl.loop(0, bins // CFAR_ROWS)
    def _(i):
        start = pl.multiple_of(i * CFAR_ROWS, CFAR_ROWS)
        x = power[pl.ds(start, CFAR_ROWS + 2 * ROW_PAD), :]
        two = x + shifted(x, 1, 1)
        four = two + shifted(two, 2, 1)
        eight = four + shifted(four, 4, 1)
        sixteen = eight + shifted(eight, 8, 1)
        wide = sixteen + shifted(sixteen, 16, 1) + shifted(x, 32, 1)
        wide = shifted(wide, -(WIN_R // 2), 1)[:, :cells]
        guard = (shifted(four, -2, 1) + shifted(x, 2, 1))[:, :cells]
        pair = wide + shifted(wide, 1, 0)
        quad = pair + shifted(pair, 2, 0)
        nine = quad + shifted(quad, 4, 0) + shifted(wide, 8, 0)
        three = guard + shifted(guard, 1, 0) + shifted(guard, 2, 0)
        train = shifted(nine, ROW_PAD - WIN_D // 2, 0) - shifted(three, ROW_PAD - GUARD_D // 2, 0)
        noise = train[:CFAR_ROWS] * inverse_count
        out_ref[pl.ds(start, CFAR_ROWS), :] = x[ROW_PAD : ROW_PAD + CFAR_ROWS, :cells] / noise

    @pl.when(has_left)
    def _():
        edge_copy(0).wait_send()

    @pl.when(has_right)
    def _():
        edge_copy(1).wait_send()


def solution(mesh):
    n = mesh.shape["rng"]

    def local(echoes, phase_code):
        _, local_pulses, all_cells = echoes.shape
        rows, pulses, cells = 2 * local_pulses, n * local_pulses, all_cells // n
        taps = phase_code.shape[0]
        group = pulses // PACK
        table = jnp.asarray(doppler_table(pulses, local_pulses))
        vmem = pl.BlockSpec(memory_space=pltpu.VMEM)
        hbm = pl.BlockSpec(memory_space=pl.ANY)
        return pl.pallas_call(
            functools.partial(body, n),
            out_shape=jax.ShapeDtypeStruct((pulses, cells), jnp.float32),
            in_specs=[hbm, vmem, hbm],
            out_specs=vmem,
            scratch_shapes=[
                pltpu.VMEM((rows, all_cells + taps), jnp.bfloat16),
                pltpu.VMEM((2 * pulses, 2 * pulses), jnp.bfloat16),
                pltpu.VMEM((2 * taps, taps), jnp.bfloat16),
                pltpu.VMEM((n, rows, cells), jnp.bfloat16),
                pltpu.VMEM((n, rows, cells), jnp.bfloat16),
                pltpu.VMEM((pulses + 2 * ROW_PAD, cells + LANES), jnp.float32),
                pltpu.VMEM((2, group, LANES), jnp.float32),
                pltpu.VMEM((2, group, LANES), jnp.float32),
                pltpu.SemaphoreType.DMA,
                pltpu.SemaphoreType.DMA,
                pltpu.SemaphoreType.DMA((n,)),
                pltpu.SemaphoreType.DMA((n,)),
                pltpu.SemaphoreType.DMA((2,)),
                pltpu.SemaphoreType.DMA((2,)),
            ],
            compiler_params=pltpu.CompilerParams(
                collective_id=0, has_side_effects=True, vmem_limit_bytes=48 << 20
            ),
        )(echoes.reshape(rows, all_cells), phase_code.reshape(1, taps), table)

    return jax.shard_map(
        local, mesh=mesh, in_specs=(P("beam", "rng", None), P()), out_specs=P("beam", "rng"), check_vma=False
    )
```

time: 182 us -> 80.4 us (0.44)
  Pallas kernels: 0 us -> 75.7 us
  local copies, waits for them, and re-layouts: 64.4 us -> 3.59 us
  other arithmetic: 55.1 us -> 0 us
  waiting for transfers between devices: 32.5 us -> 0 us
  matrix products: 16.1 us -> 0 us
  starting transfers between devices: 12.3 us -> 0 us
    pallas_call x0 -> x1, Pallas kernels: none -> 75.7 us  [local(): pl.pallas_call(functools.partial(body, n), out_shape=jax.ShapeDtypeStruct...]
    all_to_all x1 -> x0, waiting for transfers between devices: 28.3 us -> none  [corner_turn(): lax.all_to_all(signal, 'rng', split_axis=2, concat_axis=1, tiled=True)]
    another operation x1 -> x0, other arithmetic: 19 us -> none
    div x1 -> x0, other arithmetic: 18.1 us -> none  [cfar_ratio(): return center_power / noise_level]
    dot_general x4 -> x0, matrix products: 16.1 us -> none  [the longest x1 10.6 us: power_of(): spectrum = jnp.dot(table, stacked, preferred_element_type=jnp.float32)]
    unnamed x6 -> x5, local copies, waits for them, and re-layouts: 15.2 us -> 3.59 us
    dot_general x2 -> x0, local copies, waits for them, and re-layouts: 11.2 us -> none  [the longest x1 5.61 us: compress_rows(): jnp.dot(block_rows, lower_half, preferred_element_type=jnp.float32)]
    add x3 -> x0, other arithmetic: 10.4 us -> none  [the longest x2 10 us: range_sums(): running = running + padded[..., offset:offset + cell_count]]
  transfers between devices with their start and end apart: 3 -> 0, of which waited for: 2 -> 0; matrix products, arithmetic and copies ran while one was open for 11% -> 0% of each run, Pallas kernels for 0% -> 0%
where the time goes in v1:
time: 80.4 us; the launch traced here: 79.3 us
  Pallas kernels  75.7 us (94%)
  local copies, waits for them, and re-layouts  3.59 us (4%)
    pallas_call x1, Pallas kernels, local(): pl.pallas_call(functools.partial(body, n), out_shape=jax.ShapeDtypeStruct...  75.7 us
    unnamed x5, local copies, waits for them, and re-layouts  3.59 us

profile of v1, /device:TPU:13, one launch (start us, length us, event | category | flops | bytes accessed | tf_op | source)
XLA Modules:
  0.0 79.3 jit_solution(16437877364457823064)
XLA Ops:
  0.0 0.0 copy-start
  0.0 1.6 %copy-done = bf16[2,64,8192]{2,1,0:T(8,128)(2,1)S(1)} copy-done((bf16[2,64,8192]{2,1,0:T(8,128)(2,1)S(1)}, bf16[2,64,8192]{2,1,0:T(8,128)(2,1)}, u32[]{:S(2)}) %copy-start) | copy-done | bytes 2097176
  1.6 0.0 copy-start.1
  1.6 0.7 copy-done.1
  2.3 75.7 %shard_map.37 = f32[1024,512]{1,0:T(8,128)S(1)} custom-call(bf16[128,8192]{1,0:T(8,128)(2,1)S(1)} %bitcast.2, s32[1,256]{1,0:T(1,128)S(1)} %bitcast.3, bf16[2048,2048]{1,0:T(8,128)(2,1)} %constant.2.clone.table_hbm), custom_call_target="tpu_custom_call" | custom-call | tf_op jit(solution)/shard_map/pallas_call | solution.py:235
  77.9 1.3 %copy.5 = f32[1024,512]{1,0:T(8,128)} copy(f32[1024,512]{1,0:T(8,128)S(1)} %shard_map.37) | data formatting | bytes 4194304
Async XLA Ops:
  0.0 1.6 %copy-start = (bf16[2,64,8192]{2,1,0:T(8,128)(2,1)S(1)}, bf16[2,64,8192]{2,1,0:T(8,128)(2,1)}, u32[]{:S(2)}) copy-start(bf16[2,64,8192]{2,1,0:T(8,128)(2,1)} %param.3) | copy-start | bytes 6291460
  1.6 0.7 copy-start.1

commit v2 on v1

v2 whole, which is shorter than its diff:
```python
import functools
import math

import jax
import jax.numpy as jnp
import numpy as np
from jax import lax
from jax.experimental import pallas as pl
from jax.experimental.pallas import tpu as pltpu
from jax.sharding import PartitionSpec as P

WIN_R = 33
WIN_D = 9
GUARD_R = 5
GUARD_D = 3
LANES = 128
HALO = WIN_R // 2
PACK = LANES // HALO
ROW_PAD = 16
CFAR_ROWS = 128
MESH = pl.DeviceIdType.MESH


def doppler_rows(pulses, local_pulses):
    step = np.float32(2.0 * math.pi / pulses)
    index_all = np.arange(pulses, dtype=np.int64)
    bins = np.arange(pulses // 4, dtype=np.int64)
    angle = (bins[:, None] * index_all[None, :] % pulses).astype(np.float32) * step
    taper = np.float32(0.5) - np.float32(0.5) * np.cos((index_all.astype(np.float32) + np.float32(0.5)) * step)
    cosine = taper[None, :] * np.cos(angle)
    sine = taper[None, :] * np.sin(angle)
    table = np.block([[cosine, sine], [-sine, cosine]]).astype(jnp.bfloat16)
    table = table.reshape(pulses // 2, 2, pulses // local_pulses, local_pulses)
    return table.transpose(0, 2, 1, 3).reshape(pulses // 2, 2 * pulses)


def shifted(x, count, axis):
    size = x.shape[axis]
    return pltpu.roll(x, (-count) % size, axis)


def body(
    n, echoes_hbm, code_hbm, rows_hbm, out_ref,
    echoes, code, first_rows, table, filters, bands, outer_out, inner_out, outer_in, inner_in,
    power, high, low, edge_out, edge_in,
    echo_sem, code_sem, table_sem, outer_send, outer_recv, inner_send, inner_recv, edge_send_sem, edge_recv_sem,
):
    me = lax.axis_index("rng")
    taps = code.shape[1]
    rows, all_cells = echoes_hbm.shape
    cells = all_cells // n
    blocks = cells // taps
    bins = table.shape[0] // 2
    tile = bins // 4
    half = LANES

    echo_copy = pltpu.make_async_copy(echoes_hbm, echoes.at[:, pl.ds(0, all_cells)], echo_sem)
    echo_copy.start()
    code_copy = pltpu.make_async_copy(code_hbm, code, code_sem)
    code_copy.start()
    table_copy = pltpu.make_async_copy(rows_hbm, first_rows, table_sem)
    table_copy.start()

    barrier = pltpu.get_barrier_semaphore()

    @pl.loop(1, n)
    def _(k):
        pl.semaphore_signal(barrier, inc=1, device_id={"rng": lax.rem(me + k, n)}, device_id_type=MESH)

    code_copy.wait()
    row = lax.broadcasted_iota(jnp.int32, (taps, taps), 0)
    col = lax.broadcasted_iota(jnp.int32, (taps, taps), 1)
    rolled = jnp.broadcast_to(code[...].astype(jnp.float32), (taps, taps))
    for bit in range((taps - 1).bit_length()):
        rolled = jnp.where((row & (1 << bit)) != 0, pltpu.roll(rolled, 1 << bit, 1), rolled)
    circulant = rolled.T
    filters[pl.ds(0, taps), :] = jnp.where(row >= col, circulant, 0.0).astype(jnp.bfloat16)
    filters[pl.ds(taps, taps), :] = jnp.where(row < col, circulant, 0.0).astype(jnp.bfloat16)
    echoes[:, pl.ds(all_cells, taps)] = jnp.zeros((rows, taps), jnp.bfloat16)

    echo_copy.wait()
    pl.semaphore_wait(barrier, n - 1)

    def compressed(owner):
        parts = [
            echoes[:, pl.ds(pl.multiple_of(owner * cells + b * taps, taps), taps)] for b in range(blocks + 1)
        ]
        pairs = jnp.concatenate(
            [jnp.concatenate(parts[:-1], axis=0), jnp.concatenate(parts[1:], axis=0)], axis=1
        )
        made = jnp.dot(pairs, filters[...], preferred_element_type=jnp.float32).astype(jnp.bfloat16)
        return [made[b * rows : (b + 1) * rows] for b in range(blocks)]

    def outer_copy(slot, owner):
        return pltpu.make_async_remote_copy(
            src_ref=outer_out.at[owner],
            dst_ref=outer_in.at[slot],
            send_sem=outer_send.at[owner],
            recv_sem=outer_recv.at[slot],
            device_id={"rng": owner},
            device_id_type=MESH,
        )

    def inner_copy(slot, owner):
        return pltpu.make_async_remote_copy(
            src_ref=inner_out.at[owner],
            dst_ref=inner_in.at[slot],
            send_sem=inner_send.at[owner],
            recv_sem=inner_recv.at[slot],
            device_id={"rng": owner},
            device_id_type=MESH,
        )

    def place(outer, inner, slot, parts):
        left, right = parts
        outer[slot, :, :half] = left[:, :half]
        outer[slot, :, half:] = right[:, half:]
        inner[slot, :, :half] = left[:, half:]
        inner[slot, :, half:] = right[:, :half]

    @pl.loop(1, n)
    def _(k):
        owner = lax.rem(me + k, n)
        place(outer_out, inner_out, owner, compressed(owner))
        outer_copy(me, owner).start()

    @pl.loop(1, n)
    def _(k):
        inner_copy(me, lax.rem(me + k, n)).start()

    place(outer_in, inner_in, me, compressed(me))

    table_copy.wait()
    column = lax.broadcasted_iota(jnp.int32, (1, 2 * bins), 1)
    for quarter in range(4):
        turn = (column * quarter) % 4
        same = jnp.where(turn == 0, 1.0, jnp.where(turn == 2, -1.0, 0.0)).astype(jnp.bfloat16)
        other = jnp.where(turn == 1, 1.0, jnp.where(turn == 3, -1.0, 0.0)).astype(jnp.bfloat16)

        @pl.loop(0, tile // 32)
        def _(j):
            start = pl.multiple_of(j * 32, 32)
            real = first_rows[pl.ds(start, 32), :]
            imag = first_rows[pl.ds(pl.multiple_of(start + tile, 32), 32), :]
            base = quarter * 2 * tile
            table[pl.ds(pl.multiple_of(base + start, 32), 32), :] = real * same + imag * other
            table[pl.ds(pl.multiple_of(base + tile + start, 32), 32), :] = imag * same - real * other

    distance = (
        lax.broadcasted_iota(jnp.int32, (4 * half, 2 * half), 0)
        - half
        - lax.broadcasted_iota(jnp.int32, (4 * half, 2 * half), 1)
    )
    for side, width in ((0, WIN_R), (1, GUARD_R)):
        band = jnp.where(jnp.abs(distance) <= width // 2, 1.0, 0.0).astype(jnp.bfloat16)
        for part in range(2):
            bands[part * 4 * half : (part + 1) * 4 * half, side * 2 * half : (side + 1) * 2 * half] = band

    def keep(start, count, lane_tile, value):
        power[pl.ds(start, count), lane_tile * LANES : (lane_tile + 1) * LANES] = value
        top = value.astype(jnp.bfloat16)
        rest = (value - top.astype(jnp.float32)).astype(jnp.bfloat16)
        for at in ((lane_tile + 1,) if lane_tile < 4 else (0, 5)):
            high[pl.ds(start, count), at * LANES : (at + 1) * LANES] = top
            low[pl.ds(start, count), at * LANES : (at + 1) * LANES] = rest

    def transform(held, lane_tiles):
        signal = held[...].reshape(n * rows, 2 * half)

        @pl.loop(0, 4)
        def _(i):
            made = jnp.dot(
                table[pl.ds(pl.multiple_of(i * 2 * tile, 2 * tile), 2 * tile), :],
                signal,
                preferred_element_type=jnp.float32,
            )
            real, imag = made[:tile], made[tile:]
            value = real * real + imag * imag
            start = pl.multiple_of(i * tile + ROW_PAD, ROW_PAD)
            keep(start, tile, lane_tiles[0], value[:, :half])
            keep(start, tile, lane_tiles[1], value[:, half:])

    @pl.loop(1, n)
    def _(k):
        outer_copy(lax.rem(me + n - k, n), lax.rem(me + k, n)).wait()

    transform(outer_in, (0, 3))

    group = bins // PACK
    lane = lax.broadcasted_iota(jnp.int32, (group, LANES), 1)

    def packed(first, turn):
        total = jnp.zeros((group, LANES), jnp.float32)
        for g in range(PACK):
            held = power[pl.ds(ROW_PAD + g * group, group), pl.ds(first, LANES)]
            total = jnp.where(lane // HALO == g, pltpu.roll(held, (g * HALO + turn) % LANES, 1), total)
        return total

    edge_out[0] = packed(0, 0)
    edge_out[1] = packed(cells - LANES, HALO)

    def edge_copy(side):
        return pltpu.make_async_remote_copy(
            src_ref=edge_out.at[side],
            dst_ref=edge_in.at[side],
            send_sem=edge_send_sem.at[side],
            recv_sem=edge_recv_sem.at[side],
            device_id={"rng": lax.rem(me + (n - 1 if side == 0 else 1), n)},
            device_id_type=MESH,
        )

    has_left, has_right = me > 0, me < n - 1

    @pl.when(has_left)
    def _():
        edge_copy(0).start()

    @pl.when(has_right)
    def _():
        edge_copy(1).start()

    @pl.when(has_right)
    def _():
        edge_copy(0).wait_recv()

    @pl.when(jnp.logical_not(has_right))
    def _():
        edge_in[0] = jnp.zeros((group, LANES), jnp.float32)

    @pl.when(has_left)
    def _():
        edge_copy(1).wait_recv()

    @pl.when(jnp.logical_not(has_left))
    def _():
        edge_in[1] = jnp.zeros((group, LANES), jnp.float32)

    after, before = edge_in[0], edge_in[1]
    for g in range(PACK):
        ends = jnp.where(
            lane < HALO,
            pltpu.roll(after, (-g * HALO) % LANES, 1),
            jnp.where(lane >= LANES - HALO, pltpu.roll(before, (-g * HALO - HALO) % LANES, 1), 0.0),
        )
        keep(ROW_PAD + g * group, group, 4, ends)

    @pl.loop(1, n)
    def _(k):
        inner_copy(lax.rem(me + n - k, n), lax.rem(me + k, n)).wait()

    transform(inner_in, (1, 2))
    for ref in (high, low):
        ref[pl.ds(0, ROW_PAD), :] = ref[pl.ds(bins, ROW_PAD), :]
        ref[pl.ds(bins + ROW_PAD, ROW_PAD), :] = ref[pl.ds(ROW_PAD, ROW_PAD), :]

    position = me * cells + lax.broadcasted_iota(jnp.int32, (1, cells), 1)

    def inside(half):
        return jnp.minimum(position + half, all_cells - 1) - jnp.maximum(position - half, 0) + 1

    count = inside(WIN_R // 2) * WIN_D - inside(GUARD_R // 2) * GUARD_D
    inverse_count = 1.0 / count.astype(jnp.float32)

    @pl.loop(0, bins // CFAR_ROWS)
    def _(i):
        start = pl.multiple_of(i * CFAR_ROWS, CFAR_ROWS)
        span = CFAR_ROWS + 2 * ROW_PAD
        center = power[pl.ds(pl.multiple_of(start + ROW_PAD, ROW_PAD), CFAR_ROWS), :]
        for side in range(2):
            lanes = slice(side * 2 * half, side * 2 * half + 4 * half)
            both = jnp.concatenate([high[pl.ds(start, span), lanes], low[pl.ds(start, span), lanes]], axis=1)
            sums = jnp.dot(both, bands[...], preferred_element_type=jnp.float32)
            wide, guard = sums[:, : 2 * half], sums[:, 2 * half :]
            pair = wide + shifted(wide, 1, 0)
            quad = pair + shifted(pair, 2, 0)
            nine = quad + shifted(quad, 4, 0) + shifted(wide, 8, 0)
            three = guard + shifted(guard, 1, 0) + shifted(guard, 2, 0)
            train = shifted(nine, ROW_PAD - WIN_D // 2, 0) - shifted(three, ROW_PAD - GUARD_D // 2, 0)
            own = slice(side * 2 * half, (side + 1) * 2 * half)
            noise = train[:CFAR_ROWS] * inverse_count[:, own]
            out_ref[pl.ds(start, CFAR_ROWS), own] = center[:, own] / noise

    @pl.when(has_left)
    def _():
        edge_copy(0).wait_send()

    @pl.when(has_right)
    def _():
        edge_copy(1).wait_send()


def solution(mesh):
    n = mesh.shape["rng"]

    def local(echoes, phase_code):
        _, local_pulses, all_cells = echoes.shape
        rows, pulses, cells = 2 * local_pulses, n * local_pulses, all_cells // n
        taps = phase_code.shape[0]
        group = pulses // PACK
        if cells != 2 * taps or cells != 4 * LANES or local_pulses % 4:
            raise ValueError("unsupported shape")
        hbm = pl.BlockSpec(memory_space=pl.ANY)
        return pl.pallas_call(
            functools.partial(body, n),
            out_shape=jax.ShapeDtypeStruct((pulses, cells), jnp.float32),
            in_specs=[hbm, hbm, hbm],
            out_specs=pl.BlockSpec(memory_space=pltpu.VMEM),
            scratch_shapes=[
                pltpu.VMEM((rows, all_cells + taps), jnp.bfloat16),
                pltpu.VMEM((1, taps), jnp.int32),
                pltpu.VMEM((pulses // 2, 2 * pulses), jnp.bfloat16),
                pltpu.VMEM((2 * pulses, 2 * pulses), jnp.bfloat16),
                pltpu.VMEM((2 * taps, taps), jnp.bfloat16),
                pltpu.VMEM((8 * LANES, 4 * LANES), jnp.bfloat16),
                pltpu.VMEM((n, rows, 2 * LANES), jnp.bfloat16),
                pltpu.VMEM((n, rows, 2 * LANES), jnp.bfloat16),
                pltpu.VMEM((n, rows, 2 * LANES), jnp.bfloat16),
                pltpu.VMEM((n, rows, 2 * LANES), jnp.bfloat16),
                pltpu.VMEM((pulses + 2 * ROW_PAD, cells + LANES), jnp.float32),
                pltpu.VMEM((pulses + 2 * ROW_PAD, cells + 2 * LANES), jnp.bfloat16),
                pltpu.VMEM((pulses + 2 * ROW_PAD, cells + 2 * LANES), jnp.bfloat16),
                pltpu.VMEM((2, group, LANES), jnp.float32),
                pltpu.VMEM((2, group, LANES), jnp.float32),
                pltpu.SemaphoreType.DMA,
                pltpu.SemaphoreType.DMA,
                pltpu.SemaphoreType.DMA,
                pltpu.SemaphoreType.DMA((n,)),
                pltpu.SemaphoreType.DMA((n,)),
                pltpu.SemaphoreType.DMA((n,)),
                pltpu.SemaphoreType.DMA((n,)),
                pltpu.SemaphoreType.DMA((2,)),
                pltpu.SemaphoreType.DMA((2,)),
            ],
            compiler_params=pltpu.CompilerParams(
                collective_id=0, has_side_effects=True, vmem_limit_bytes=60 << 20
            ),
        )(echoes.reshape(rows, all_cells), phase_code.reshape(1, taps),
          jnp.asarray(doppler_rows(pulses, local_pulses)))

    return jax.shard_map(
        local, mesh=mesh, in_specs=(P("beam", "rng", None), P()), out_specs=P("beam", "rng"), check_vma=False
    )
```

time: 80.4 us -> 65.2 us (0.81); the launches traced: 79.3 us -> 65.1 us
  Pallas kernels: 75.7 us -> 62 us
    pallas_call x1, Pallas kernels: 75.7 us -> 62 us  [local(): pl.pallas_call(functools.partial(body, n), out_shape=jax.ShapeDtypeStruct...]
    unnamed x5 -> x1, local copies, waits for them, and re-layouts: 3.59 us -> 3.08 us
where the time goes in v2:
time: 65.2 us; the launch traced here: 65.1 us
  Pallas kernels  62 us (95%)
  local copies, waits for them, and re-layouts  3.08 us (5%)
    pallas_call x1, Pallas kernels, local(): pl.pallas_call(functools.partial(body, n), out_shape=jax.ShapeDtypeStruct...  62 us
    unnamed x1, local copies, waits for them, and re-layouts  3.08 us

profile of v2, /device:TPU:13, one launch (start us, length us, event | category | flops | bytes accessed | tf_op | source)
XLA Modules:
  0.0 65.1 jit_solution(669998678114777036)
XLA Ops:
  0.0 62.0 %shard_map.37 = f32[1024,512]{1,0:T(8,128)} custom-call(bf16[128,8192]{1,0:T(8,128)(2,1)} %bitcast.2, s32[1,256]{1,0:T(1,128)} %bitcast.3, bf16[512,2048]{1,0:T(8,128)(2,1)} %constant.2.clone.rows_hbm), custom_call_target="tpu_custom_call" | custom-call | tf_op jit(solution)/shard_map/pallas_call | solution.py:303
  62.0 3.1 %copy.5 = f32[1024,512]{1,0:T(8,128)} copy(f32[1024,512]{1,0:T(8,128)} %shard_map.37) | data formatting | bytes 4194304

commit v3 on v2

--- a/solution.py
+++ b/solution.py
@@ -17,7 +17,7 @@
 HALO = WIN_R // 2
 PACK = LANES // HALO
 ROW_PAD = 16
-CFAR_ROWS = 128
+CFAR_ROWS = 256
 MESH = pl.DeviceIdType.MESH
 
 
@@ -40,10 +40,10 @@
 
 
 def body(
-    n, echoes_hbm, code_hbm, rows_hbm, out_ref,
+    n, echoes_hbm, code_hbm, rows_hbm, out_hbm,
     echoes, code, first_rows, table, filters, bands, outer_out, inner_out, outer_in, inner_in,
-    power, high, low, edge_out, edge_in,
-    echo_sem, code_sem, table_sem, outer_send, outer_recv, inner_send, inner_recv, edge_send_sem, edge_recv_sem,
+    power, high, low, result, edge_out, edge_in,
+    echo_sem, code_sem, table_sem, outer_send, outer_recv, inner_send, inner_recv, edge_send_sem, edge_recv_sem, result_sem,
 ):
     me = lax.axis_index("rng")
     taps = code.shape[1]
@@ -167,18 +167,21 @@
     def transform(held, lane_tiles):
         signal = held[...].reshape(n * rows, 2 * half)
 
-        @pl.loop(0, 4)
+        together = 2
+
+        @pl.loop(0, 4 // together)
         def _(i):
+            size = 2 * together * tile
             made = jnp.dot(
-                table[pl.ds(pl.multiple_of(i * 2 * tile, 2 * tile), 2 * tile), :],
-                signal,
-                preferred_element_type=jnp.float32,
+                table[pl.ds(pl.multiple_of(i * size, size), size), :], signal, preferred_element_type=jnp.float32
             )
-            real, imag = made[:tile], made[tile:]
-            value = real * real + imag * imag
-            start = pl.multiple_of(i * tile + ROW_PAD, ROW_PAD)
-            keep(start, tile, lane_tiles[0], value[:, :half])
-            keep(start, tile, lane_tiles[1], value[:, half:])
+            for t in range(together):
+                real = made[2 * t * tile : (2 * t + 1) * tile]
+                imag = made[(2 * t + 1) * tile : (2 * t + 2) * tile]
+                value = real * real + imag * imag
+                start = pl.multiple_of((i * together + t) * tile + ROW_PAD, ROW_PAD)
+                keep(start, tile, lane_tiles[0], value[:, :half])
+                keep(start, tile, lane_tiles[1], value[:, half:])
 
     @pl.loop(1, n)
     def _(k):
@@ -260,6 +263,10 @@
 
     count = inside(WIN_R // 2) * WIN_D - inside(GUARD_R // 2) * GUARD_D
     inverse_count = 1.0 / count.astype(jnp.float32)
+
+    def result_copy(i):
+        own = pl.ds(pl.multiple_of(i * CFAR_ROWS, CFAR_ROWS), CFAR_ROWS)
+        return pltpu.make_async_copy(result.at[own, :], out_hbm.at[own, :], result_sem.at[i])
 
     @pl.loop(0, bins // CFAR_ROWS)
     def _(i):
@@ -278,7 +285,8 @@
             train = shifted(nine, ROW_PAD - WIN_D // 2, 0) - shifted(three, ROW_PAD - GUARD_D // 2, 0)
             own = slice(side * 2 * half, (side + 1) * 2 * half)
             noise = train[:CFAR_ROWS] * inverse_count[:, own]
-            out_ref[pl.ds(start, CFAR_ROWS), own] = center[:, own] / noise
+            result[pl.ds(start, CFAR_ROWS), own] = center[:, own] / noise
+        result_copy(i).start()
 
     @pl.when(has_left)
     def _():
@@ -287,6 +295,10 @@
     @pl.when(has_right)
     def _():
         edge_copy(1).wait_send()
+
+    @pl.loop(0, bins // CFAR_ROWS)
+    def _(i):
+        result_copy(i).wait()
 
 
 def solution(mesh):
@@ -304,7 +316,7 @@
             functools.partial(body, n),
             out_shape=jax.ShapeDtypeStruct((pulses, cells), jnp.float32),
             in_specs=[hbm, hbm, hbm],
-            out_specs=pl.BlockSpec(memory_space=pltpu.VMEM),
+            out_specs=hbm,
             scratch_shapes=[
                 pltpu.VMEM((rows, all_cells + taps), jnp.bfloat16),
                 pltpu.VMEM((1, taps), jnp.int32),
@@ -319,6 +331,7 @@
                 pltpu.VMEM((pulses + 2 * ROW_PAD, cells + LANES), jnp.float32),
                 pltpu.VMEM((pulses + 2 * ROW_PAD, cells + 2 * LANES), jnp.bfloat16),
                 pltpu.VMEM((pulses + 2 * ROW_PAD, cells + 2 * LANES), jnp.bfloat16),
+                pltpu.VMEM((pulses, cells), jnp.float32),
                 pltpu.VMEM((2, group, LANES), jnp.float32),
                 pltpu.VMEM((2, group, LANES), jnp.float32),
                 pltpu.SemaphoreType.DMA,
@@ -330,6 +343,7 @@
                 pltpu.SemaphoreType.DMA((n,)),
                 pltpu.SemaphoreType.DMA((2,)),
                 pltpu.SemaphoreType.DMA((2,)),
+                pltpu.SemaphoreType.DMA((pulses // CFAR_ROWS,)),
             ],
             compiler_params=pltpu.CompilerParams(
                 collective_id=0, has_side_effects=True, vmem_limit_bytes=60 << 20

time: 65.2 us -> 63.9 us (0.980)
  Pallas kernels: 62 us -> 60.7 us
    pallas_call x1, Pallas kernels: 62 us -> 60.7 us  [local(): pl.pallas_call(functools.partial(body, n), out_shape=jax.ShapeDtypeStruct...]
where the time goes in v3:
time: 63.9 us; the launch traced here: 63.8 us
  Pallas kernels  60.7 us (95%)
  local copies, waits for them, and re-layouts  3.08 us (5%)
    pallas_call x1, Pallas kernels, local(): pl.pallas_call(functools.partial(body, n), out_shape=jax.ShapeDtypeStruct...  60.7 us
    unnamed x1, local copies, waits for them, and re-layouts  3.08 us

profile of v3, /device:TPU:13, one launch (start us, length us, event | category | flops | bytes accessed | tf_op | source)
XLA Modules:
  0.0 63.8 jit_solution(17008540436140707412)
XLA Ops:
  0.0 60.7 %shard_map.37 = f32[1024,512]{1,0:T(8,128)} custom-call(bf16[128,8192]{1,0:T(8,128)(2,1)} %bitcast.2, s32[1,256]{1,0:T(1,128)} %bitcast.3, bf16[512,2048]{1,0:T(8,128)(2,1)} %constant.2.clone.rows_hbm), custom_call_target="tpu_custom_call" | custom-call | tf_op jit(solution)/shard_map/pallas_call | solution.py:315
  60.7 3.1 %copy.5 = f32[1024,512]{1,0:T(8,128)} copy(f32[1024,512]{1,0:T(8,128)} %shard_map.37) | data formatting | bytes 4194304
